TPU v7x, 32 devices: a whole 2x2x4 slice. The times are simulated.
32 devices in a mesh: groups: 2 (over y), slab: 4 (over z), batch: 2 (over x), chan: 2 (over core).
Axes of the slice: x: 2, y: 2, z: 4, core: 2. Of those that a mesh axis runs over, the one named last changes fastest.
Arguments:
- volume: bfloat16 [16, 8, 4, 8, 128], P(('groups', 'batch'), 'slab'), parts along dimension 0, may hold values from -6 to 6
- targets: float32 [16, 4], P(('groups', 'batch')), parts along dimension 0, may hold values from -1 to 1
- front_weight: bfloat16 [3, 3, 3, 128, 128], P(None, None, None, None, 'chan'), may hold values from -0.109375 to 0.109375
- stride_weight: bfloat16 [3, 3, 3, 128, 256], P(None, None, None, 'chan'), may hold values from -0.109375 to 0.109375
- hidden_weight: float32 [256, 128], P('chan'), may hold values from -0.375 to 0.375
- output_weight: float32 [128, 4], replicated, may hold values from -0.5 to 0.5
Outputs:
- grad_front: float32 [6, 3, 3, 128, 128], P('groups', None, None, None, 'chan'), parts along dimension 0
- grad_stride: float32 [6, 3, 3, 128, 256], P('groups', None, None, 'chan'), parts along dimension 0
- grad_hidden: float32 [512, 128], P(('groups', 'chan')), parts along dimension 0
- grad_output: float32 [256, 4], P('groups'), parts along dimension 0
- loss: float32 [2], P('groups'), parts along dimension 0
There are 2 independent parts, one for each index of `groups`. A program takes and returns all parts, laid end to end along the dimension named above; an argument that names none is the same for every part. Nothing has to cross between parts.
All inputs are finite; a program needn't handle non-finite values.
Results may differ from a plain program's by a relative error of at most 0.0052.
Values may be sent and summed in bfloat16 or wider, within the bound.
A program may use at most 64 MiB of HBM per device.

v0:
```python
import jax
import jax.numpy as jnp
from jax import lax
from jax.sharding import PartitionSpec as P


def with_halo(cells, sides, width):
    for axis, dim in sides:
        count = lax.axis_size(axis)
        ends = count - 1
        head = lax.slice_in_dim(cells, 0, width, axis=dim)
        tail = lax.slice_in_dim(cells, cells.shape[dim] - width, cells.shape[dim], axis=dim)
        cells = jnp.concatenate(
            [
                lax.ppermute(tail, axis, [(i, (i + 1) % count) for i in range(ends)]),
                cells,
                lax.ppermute(head, axis, [((i + 1) % count, i) for i in range(ends)]),
            ],
            axis=dim,
        )
    return cells


def swish_slope(preact):
    logistic = jax.nn.sigmoid(preact)
    return logistic * (1.0 + preact * (1.0 - logistic))


def tap_window(padded, tap_z, tap_x, tap_y, extent_z, extent_x, extent_y, stride):
    if stride == 1:
        return padded[
            :, tap_z : tap_z + extent_z, tap_x : tap_x + extent_x, tap_y : tap_y + extent_y, :
        ]
    leading = padded.shape[0]
    channels = padded.shape[-1]
    folded = padded.reshape(leading, extent_z + 1, 2, extent_x + 1, 2, extent_y + 1, 2, channels)
    return folded[
        :,
        tap_z // 2 : tap_z // 2 + extent_z,
        tap_z % 2,
        tap_x // 2 : tap_x // 2 + extent_x,
        tap_x % 2,
        tap_y // 2 : tap_y // 2 + extent_y,
        tap_y % 2,
        :,
    ]


def conv_apply(padded, weight, extent_z, extent_x, extent_y, stride):
    summed = None
    for tap_z in range(3):
        for tap_x in range(3):
            for tap_y in range(3):
                window = tap_window(
                    padded, tap_z, tap_x, tap_y, extent_z, extent_x, extent_y, stride
                )
                flat_tap = window.reshape(-1, window.shape[-1])
                contrib = jnp.dot(
                    flat_tap, weight[tap_z, tap_x, tap_y], preferred_element_type=jnp.float32
                )
                summed = contrib if summed is None else summed + contrib
    return summed.reshape(padded.shape[0], extent_z, extent_x, extent_y, weight.shape[-1])


def kernel_grad(padded, grad_out, extent_z, extent_x, extent_y, stride):
    flat_grad = grad_out.reshape(-1, grad_out.shape[-1])
    results = []
    for tap_z in range(3):
        for tap_x in range(3):
            for tap_y in range(3):
                window = tap_window(
                    padded, tap_z, tap_x, tap_y, extent_z, extent_x, extent_y, stride
                )
                flat_tap = window.reshape(-1, window.shape[-1])
                results.append(
                    lax.dot_general(
                        flat_tap,
                        flat_grad,
                        (((0,), (0,)), ((), ())),
                        preferred_element_type=jnp.float32,
                    )
                )
    return jnp.stack(results).reshape(3, 3, 3, padded.shape[-1], grad_out.shape[-1])


def input_grad(grad_out, weight, extent_z, extent_x, extent_y):
    leading = grad_out.shape[0]
    channels = weight.shape[3]
    flat_grad = grad_out.reshape(-1, grad_out.shape[-1])
    buckets = {}
    for tap_z in range(3):
        for tap_x in range(3):
            for tap_y in range(3):
                contrib = lax.dot_general(
                    flat_grad,
                    weight[tap_z, tap_x, tap_y],
                    (((1,), (1,)), ((), ())),
                    preferred_element_type=jnp.float32,
                )
                contrib = contrib.reshape(leading, extent_z, extent_x, extent_y, channels)
                placed = jnp.pad(
                    contrib,
                    (
                        (0, 0),
                        (tap_z // 2, 1 - tap_z // 2),
                        (tap_x // 2, 1 - tap_x // 2),
                        (tap_y // 2, 1 - tap_y // 2),
                        (0, 0),
                    ),
                )
                parity = (tap_z % 2, tap_x % 2, tap_y % 2)
                buckets[parity] = placed if parity not in buckets else buckets[parity] + placed
    planes_z = []
    for par_z in range(2):
        planes_x = []
        for par_x in range(2):
            planes_x.append(jnp.stack([buckets[par_z, par_x, par_y] for par_y in range(2)], axis=4))
        planes_z.append(jnp.stack(planes_x, axis=3))
    assembled = jnp.stack(planes_z, axis=2)
    assembled = assembled.reshape(
        leading, 2 * extent_z + 2, 2 * extent_x + 2, 2 * extent_y + 2, channels
    )
    return assembled[:, 1:-1, 1:-1, 1:-1, :]


def body(volume, targets, front_weight, stride_weight, hidden_weight, output_weight):
    highest = lax.Precision.HIGHEST
    slabs = lax.axis_size("slab")
    batches = lax.axis_size("batch")
    inner = front_weight.shape[-1]
    leading, thick, extent_x, extent_y, channels = volume.shape
    depth = thick * slabs
    outputs = output_weight.shape[-1]
    haloed = with_halo(volume, (("slab", 1),), 1)
    padded = jnp.pad(haloed, ((0, 0), (0, 0), (1, 1), (1, 1), (0, 0)))
    front_pre = conv_apply(padded, front_weight, thick, extent_x, extent_y, 1)
    front_act = jax.nn.silu(front_pre).astype(jnp.bfloat16)
    merged = front_act.reshape(leading, thick, extent_x, extent_y * inner)
    sample_act = lax.all_to_all(merged, "slab", split_axis=0, concat_axis=1, tiled=True)
    sample_act = sample_act.reshape(1, depth, extent_x, extent_y, inner)
    half_z = depth // 2
    half_x = extent_x // 2
    half_y = extent_y // 2
    cells = half_z * half_x * half_y
    stride_pad = jnp.pad(sample_act, ((0, 0), (1, 1), (1, 1), (1, 1), (0, 0)))
    partial_pre = conv_apply(stride_pad, stride_weight, half_z, half_x, half_y, 2)
    stride_pre = lax.psum_scatter(partial_pre, "chan", scatter_dimension=4, tiled=True)
    pooled = jnp.sum(jax.nn.silu(stride_pre), axis=(0, 1, 2, 3)) / cells
    hidden_pre = lax.psum(jnp.dot(pooled, hidden_weight, precision=highest), "chan")
    hidden_act = jax.nn.silu(hidden_pre)
    predicted = jnp.dot(hidden_act, output_weight, precision=highest)
    target_row = lax.dynamic_index_in_dim(targets, lax.axis_index("slab"), 0, keepdims=False)
    residual = predicted - target_row
    squared = jnp.sum(residual * residual)
    grad_output = jnp.outer(hidden_act, residual)
    grad_hidden_pre = jnp.dot(output_weight, residual, precision=highest) * swish_slope(hidden_pre)
    grad_hidden = jnp.outer(pooled, grad_hidden_pre)
    grad_pooled = jnp.dot(hidden_weight, grad_hidden_pre, precision=highest)
    grad_stride_pre = (grad_pooled / cells * swish_slope(stride_pre)).astype(jnp.bfloat16)
    full_grad = lax.all_gather(grad_stride_pre, "chan", axis=4, tiled=True)
    grad_stride = kernel_grad(stride_pad, full_grad, half_z, half_x, half_y, 2)
    grad_act = input_grad(full_grad, stride_weight, half_z, half_x, half_y).astype(jnp.bfloat16)
    returned = lax.all_to_all(
        grad_act.reshape(1, depth, extent_x, extent_y * inner),
        "slab",
        split_axis=1,
        concat_axis=0,
        tiled=True,
    )
    returned = returned.reshape(leading, thick, extent_x, extent_y, inner)
    grad_front_pre = (returned * swish_slope(front_pre)).astype(jnp.bfloat16)
    grad_front = kernel_grad(padded, grad_front_pre, thick, extent_x, extent_y, 1)
    grad_front, grad_stride, grad_hidden, grad_output, squared = lax.psum(
        (grad_front, grad_stride, grad_hidden, grad_output, squared), ("slab", "batch")
    )
    loss = (squared / (slabs * batches * outputs)).reshape(1)
    return (grad_front, grad_stride, grad_hidden, grad_output, loss)


def solution(mesh):
    in_specs = (
        P(("groups", "batch"), "slab", None, None, None),
        P(("groups", "batch"), None),
        P(None, None, None, None, "chan"),
        P(None, None, None, "chan", None),
        P("chan", None),
        P(),
    )
    out_specs = (
        P("groups", None, None, None, "chan"),
        P("groups", None, None, "chan", None),
        P(("groups", "chan"), None),
        P("groups", None),
        P("groups"),
    )
    return jax.shard_map(body, mesh=mesh, in_specs=in_specs, out_specs=out_specs, check_vma=False)
```

profile of v0, /device:TPU:0, one launch (start us, length us, event | category | flops | bytes accessed | tf_op | source)
XLA Modules:
  0.0 213.3 jit_solution(12655027647742667064)
XLA Ops:
  7.2 0.8 fusion.298
  8.0 4.9 %collective-permute-start = (bf16[4,1,4,8,128]{4,3,2,1,0:T(8,128)(2,1)S(1)}, bf16[4,1,4,8,128]{4,3,2,1,0:T(8,128)(2,1)S(1)}, u32[]{:S(2)}, u32[]{:S(2)}) collective-permute-start(bf16[4,1,4,8,128]{4,3,2,1,0:T(8,128)(2,1)S(1)} %get-tuple-element.63), channel_id=1, source_target_pairs={{0,4},{4,8},{8,12},{1,5},{5,9},{9,13},{2,6},{6,10},{10,14},{3,7},{... | collective-permute-start | bytes 98312 | tf_op jit(solution)/shard_map/ppermute | solution.py:15
  13.0 1.4 collective-permute-start.1
  14.5 4.4 %collective-permute-done.1 = bf16[4,1,4,8,128]{4,3,2,1,0:T(8,128)(2,1)S(1)} collective-permute-done((bf16[4,1,4,8,128]{4,3,2,1,0:T(8,128)(2,1)S(1)}, bf16[4,1,4,8,128]{4,3,2,1,0:T(8,128)(2,1)S(1)}, u32[]{:S(2)}, u32[]{:S(2)}) %collective-permute-start.1) | collective-permute-done | bytes 32800 | tf_op jit(solution)/shard_map/ppermute | solution.py:17
  18.9 1.0 select_maximum_fusion
  19.9 0.2 fusion.294
  20.2 0.6 copy-done.6
  25.4 9.3 %all_to_all.8 = bf16[4,2,4,512]{3,2,1,0:T(4,128)(2,1)S(1)} all-to-all(bf16[4,2,4,512]{3,2,1,0:T(4,128)(2,1)S(1)} %fusion.65), channel_id=1, replica_groups=mesh['groups'=2,'slab'=4,'batch'=2,'chan'=2] {'slab'}, dimensions={0} | all-to-all | bytes 65536 | tf_op jit(solution)/shard_map/all_to_all | solution.py:139
  35.1 0.2 fusion.296
  39.2 0.8 copy.165
  40.0 1.9 reshape.469
  41.9 6.1 %reduce-scatter.4.cloned.1.call-done = f32[128,32]{1,0:T(8,128)} async-done(((f32[256,32]{1,0:T(8,128)}), f32[128,32]{1,0:T(8,128)}) %reduce-scatter.4.cloned.1.call-update) | async-done | bytes 16400
  48.0 1.5 reshape.470
  49.5 0.4 copy.166
  50.1 2.5 %psum.42 = f32[128]{0:T(128)S(1)} all-reduce(f32[128]{0:T(128)S(1)} %convolution_bitcast_fusion.83), channel_id=1, replica_groups=mesh['groups'=2,'slab'=4,'batch'=2,'chan'=2] {'chan'}, use_global_device_ids=true, to_apply=%region_2.3 | all-reduce | flops 128 | bytes 1024 | tf_op jit(solution)/shard_map/psum | solution.py:149
  52.6 1.4 multiply_reduce_fusion.1
  54.4 1.8 all_gather.3
  65.4 0.7 reshape.468
  66.1 4.8 %all-to-all-start.1 = ((bf16[1,8,4,512]{3,2,0,1:T(4,128)(2,1)}), bf16[1,8,4,512]{3,2,0,1:T(4,128)(2,1)S(1)}, u32[]{:S(2)}, u32[]{:S(2)}) async-start(bf16[1,8,4,512]{3,2,0,1:T(4,128)(2,1)} %reshape.468), calls=%async_computation.1 | async-start | bytes 65536 | tf_op jit(solution)/shard_map/all_to_all | solution.py:163
  71.0 0.7 broadcast_multiply_fusion
  71.7 4.9 %all-to-all-done.1 = bf16[1,8,4,512]{3,2,0,1:T(4,128)(2,1)S(1)} async-done(((bf16[1,8,4,512]{3,2,0,1:T(4,128)(2,1)}), bf16[1,8,4,512]{3,2,0,1:T(4,128)(2,1)S(1)}, u32[]{:S(2)}, u32[]{:S(2)}) %all-to-all-start.1) | async-done | bytes 32800 | tf_op jit(solution)/shard_map/all_to_all | solution.py:163
  76.8 0.2 fusion.54
  77.0 0.2 fusion.53
  77.4 0.2 fusion.51
  77.8 0.2 fusion.50
  78.0 0.2 fusion.49
  78.2 0.2 fusion.48
  78.5 0.2 fusion.47
  78.7 0.2 fusion.46
  78.9 0.2 fusion.45
  79.1 0.2 fusion.44
  79.3 0.2 fusion.43
  79.5 0.2 fusion.42
  79.7 0.2 fusion.41
  79.9 0.2 fusion.40
  80.5 0.2 fusion.37
  80.9 0.2 fusion.35
  81.1 0.2 fusion.34
  81.5 0.2 fusion.33
  81.7 0.2 fusion.32
  81.9 0.2 fusion.31
  82.1 0.2 fusion.30
  82.4 0.9 copy-done.5
  83.4 20.3 %all-reduce.29 = (f32[128,4]{0,1:T(4,128)}, f32[]{:T(128)}) all-reduce(f32[128,4]{0,1:T(4,128)S(1)} %broadcast_multiply_fusion.1, f32[]{:T(128)} %get-tuple-element.65), channel_id=1, replica_groups=mesh['groups'=2,'slab'=4,'batch'=2,'chan'=2] {'slab','batch'}, use_global_device_ids=true, to_apply=%region_6.7 | all-reduce | flops 513 | bytes 4104 | tf_op jit(solution)/shard_map/psum | solution.py:173
  104.3 96.9 %all-reduce.33.cloned.1.call-done = (f32[3,3,3,128,64]{3,4,2,1,0:T(8,128)}, f32[3,3,3,64,256]{4,3,2,1,0:T(8,128)}, f32[128,128]{1,0:T(8,128)}) async-done(((f32[3,3,3,128,64]{3,4,2,1,0:T(8,128)}, f32[3,3,3,64,256]{4,3,2,1,0:T(8,128)}, f32[128,128]{1,0:T(8,128)}), (f32[3,3,3,128,64]{3,4,2,1,0:T(8,128)}, f32[3,3,3,64,256]{4,3,2,1,0:T(8,128)}, f32[128,128]{1,0:T(8,128)})) %all-reduce.33.cloned.1.call-update) | async-done | bytes 2719760 | tf_op jit(solution)/shard_map/psum | solution.py:173
  201.2 2.3 %copy.225 = f32[3,3,3,128,64]{3,4,2,1,0:T(8,128)} copy(f32[3,3,3,128,64]{3,4,2,1,0:T(8,128)} %get-tuple-element.73) | data formatting | bytes 1769472
  203.5 1.2 copy.226
  204.7 0.6 copy.227
  (204 shorter events, 19.8 us)
Async XLA Ops:
  7.2 42.8 %copy-start = (f32[128,128]{1,0:T(8,128)S(1)}, f32[128,128]{1,0:T(8,128)}, u32[]{:S(2)}) copy-start(f32[128,128]{1,0:T(8,128)} %param.10) | copy-start | bytes 196612
  7.2 40.8 %reduce-scatter.4.cloned.1.call-start = ((), (), s32[]{:S(2)}) async-start(), calls=%async_computation.3 | async-start | bytes 196608
  8.0 6.5 %collective-permute-start = (bf16[4,1,4,8,128]{4,3,2,1,0:T(8,128)(2,1)S(1)}, bf16[4,1,4,8,128]{4,3,2,1,0:T(8,128)(2,1)S(1)}, u32[]{:S(2)}, u32[]{:S(2)}) collective-permute-start(bf16[4,1,4,8,128]{4,3,2,1,0:T(8,128)(2,1)S(1)} %get-tuple-element.63), channel_id=1, source_target_pairs={{0,4},{4,8},{8,12},{1,5},{5,9},{9,13},{2,6},{6,10},{10,14},{3,7},{... | collective-permute-start | bytes 98312 | tf_op jit(solution)/shard_map/ppermute | solution.py:15
  12.9 7.2 %copy-start.4 = (bf16[4,2,4,8,128]{4,3,2,1,0:T(8,128)(2,1)S(1)}, bf16[4,2,4,8,128]{4,3,2,1,0:T(8,128)(2,1)}, u32[]{:S(2)}) copy-start(bf16[4,2,4,8,128]{4,3,2,1,0:T(8,128)(2,1)} %param.6) | copy-start | bytes 196612
  13.0 5.9 %collective-permute-start.1 = (bf16[4,1,4,8,128]{4,3,2,1,0:T(8,128)(2,1)S(1)}, bf16[4,1,4,8,128]{4,3,2,1,0:T(8,128)(2,1)S(1)}, u32[]{:S(2)}, u32[]{:S(2)}) collective-permute-start(bf16[4,1,4,8,128]{4,3,2,1,0:T(8,128)(2,1)S(1)} %get-tuple-element.64), channel_id=1, source_target_pairs={{4,0},{8,4},{12,8},{5,1},{9,5},{13,9},{6,2},{10,6},{14,10},{7,3},{... | collective-permute-start | bytes 98312 | tf_op jit(solution)/shard_map/ppermute | solution.py:17
  19.9 1.0 copy-start.6
  24.8 10.9 %copy-start.1 = (bf16[3,3,3,64,256]{4,3,2,1,0:T(8,128)(2,1)S(1)}, bf16[3,3,3,64,256]{4,3,2,1,0:T(8,128)(2,1)}, u32[]{:S(2)}) copy-start(bf16[3,3,3,64,256]{4,3,2,1,0:T(8,128)(2,1)} %param.9) | copy-start | bytes 2654212
  39.2 13.4 %copy-start.8 = (f32[128,4]{0,1:T(4,128)S(1)}, f32[128,4]{0,1:T(4,128)}, u32[]{:S(2)}) copy-start(f32[128,4]{0,1:T(4,128)} %param.11) | copy-start | bytes 6148
  64.7 12.0 %copy-start.2 = (f32[27,64,256]{2,1,0:T(8,128)}, f32[27,64,256]{2,1,0:T(8,128)S(1)}, u32[]{:S(2)}) copy-start(f32[27,64,256]{2,1,0:T(8,128)S(1)} %fusion) | copy-start | bytes 5308420
  66.1 10.5 %all-to-all-start.1 = ((bf16[1,8,4,512]{3,2,0,1:T(4,128)(2,1)}), bf16[1,8,4,512]{3,2,0,1:T(4,128)(2,1)S(1)}, u32[]{:S(2)}, u32[]{:S(2)}) async-start(bf16[1,8,4,512]{3,2,0,1:T(4,128)(2,1)} %reshape.468), calls=%async_computation.1 | async-start | bytes 65536 | tf_op jit(solution)/shard_map/all_to_all | solution.py:163
  71.0 130.2 %all-reduce.33.cloned.1.call-start = ((), (), s32[]{:S(2)}) async-start(), calls=%async_computation.4 | async-start | bytes 5439488 | tf_op jit(solution)/shard_map/psum | solution.py:173
  82.4 0.9 copy-start.5
  201.2 2.3 %copy-start.3 = (f32[3,3,3,64,256]{4,3,2,1,0:T(8,128)S(1)}, f32[3,3,3,64,256]{4,3,2,1,0:T(8,128)}, u32[]{:S(2)}) copy-start(f32[3,3,3,64,256]{4,3,2,1,0:T(8,128)} %get-tuple-element.74) | copy-start | bytes 5308420
  203.5 1.2 copy-start.7
Sparse Core Ops, SparseCore 0:
  42.0 5.8 reduce-scatter.3
  83.4 117.7 all-reduce.32
where the time goes:
time: 214 us; the launch traced here: 213 us
  waiting for transfers between devices  112 us (52%)
  blocking collectives  33.9 us (16%)
  matrix products  23.2 us (11%)
  between operations  16.7 us (8%)
  local copies, waits for them, and re-layouts  13.5 us (6%)
  starting transfers between devices  11.2 us (5%)
  other arithmetic  2.34 us (1%)
    psum x1, waiting for transfers between devices, body(): lax.psum((grad_front, grad_stride, grad_hidden, grad_output, squared), ('...  96.9 us
    psum x1, blocking collectives, body(): lax.psum((grad_front, grad_stride, grad_hidden, grad_output, squared), ('...  20.3 us
    unnamed x27, local copies, waits for them, and re-layouts  10.4 us
    dot_general x54, matrix products, kernel_grad(): lax.dot_general(flat_tap, flat_grad, (((0,), (0,)), ((), ())), preferred_...  10.2 us
    all_to_all x1, blocking collectives, body(): lax.all_to_all(merged, 'slab', split_axis=0, concat_axis=1, tiled=True)  9.32 us
    dot_general x54, matrix products, conv_apply(): jnp.dot(flat_tap, weight[tap_z, tap_x, tap_y], preferred_element_type=jnp...  7.54 us
    unnamed x3, waiting for transfers between devices  6.09 us
    all_to_all x1, waiting for transfers between devices, body(): lax.all_to_all(grad_act.reshape(1, depth, extent_x, extent_y * inner), 's...  4.94 us
  transfers between devices with their start and end apart: 5, of which 5 were waited for; matrix products, arithmetic and copies ran while one was open for 0% of the time, Pallas kernels for 0%

commit v1 on v0

--- a/solution.py
+++ b/solution.py
@@ -1,6 +1,10 @@
+import functools
+
 import jax
 import jax.numpy as jnp
 from jax import lax
+from jax.experimental import pallas as pl
+from jax.experimental.pallas import tpu as pltpu
 from jax.sharding import PartitionSpec as P
 
 
@@ -123,7 +127,7 @@
     return assembled[:, 1:-1, 1:-1, 1:-1, :]
 
 
-def body(volume, targets, front_weight, stride_weight, hidden_weight, output_weight):
+def split_body(volume, targets, front_weight, stride_weight, hidden_weight, output_weight):
     highest = lax.Precision.HIGHEST
     slabs = lax.axis_size("slab")
     batches = lax.axis_size("batch")
@@ -177,6 +181,257 @@
     return (grad_front, grad_stride, grad_hidden, grad_output, loss)
 
 
+GATHER_LIMIT = 1 << 20
+
+
+def whole_kernel(
+    shape,
+    volume_ref, targets_ref, front_own_ref, front_other_ref, stride_ref, hidden_ref, output_ref,
+    grad_front_ref, grad_stride_ref, grad_hidden_ref, grad_output_ref, loss_ref,
+    taps_ref, front_ref, act_ref, slope_ref, strided_ref, spread_ref, grad_pre_ref,
+):
+    slabs, batches, leading, thick, extent_x, extent_y, channels, inner = shape
+    f32, bf16 = jnp.float32, jnp.bfloat16
+    highest = lax.Precision.HIGHEST
+    samples = batches * leading
+    depth = slabs * thick
+    rows = samples * extent_y
+    half_z, half_x, half_y = depth // 2, extent_x // 2, extent_y // 2
+    half_rows = samples * half_y
+    cells = half_z * half_x * half_y
+    wide = 3 * channels
+    local_rows = leading * extent_y
+
+    front_ref[:, :, :inner] = front_own_ref[...]
+    front_ref[:, :, inner:] = front_other_ref[...]
+
+    zeros = jnp.zeros((rows, wide), bf16)
+    for x in range(extent_x + 2):
+        taps_ref[0, x] = zeros
+        taps_ref[depth + 1, x] = zeros
+
+    row = lax.broadcasted_iota(jnp.int32, (rows, channels), 0)
+    first = (row & (extent_y - 1)) == 0
+    last = (row & (extent_y - 1)) == extent_y - 1
+    half_row = lax.broadcasted_iota(jnp.int32, (half_rows, channels), 0)
+    half_first = (half_row & (half_y - 1)) == 0
+    half_last = (half_row & (half_y - 1)) == half_y - 1
+
+    def fill(slab, carry):
+        for plane in range(thick):
+            z = slab * thick + plane
+            taps_ref[z + 1, 0] = zeros
+            taps_ref[z + 1, extent_x + 1] = zeros
+            for x in range(extent_x):
+                mid = jnp.concatenate(
+                    [
+                        volume_ref[b * slabs + slab, :, plane, x].astype(f32).reshape(local_rows, channels)
+                        for b in range(batches)
+                    ],
+                    axis=0,
+                )
+                low = jnp.where(first, 0.0, pltpu.roll(mid, 1, 0))
+                high = jnp.where(last, 0.0, pltpu.roll(mid, rows - 1, 0))
+                taps_ref[z + 1, x + 1, :, :channels] = low.astype(bf16)
+                taps_ref[z + 1, x + 1, :, channels : 2 * channels] = mid.astype(bf16)
+                taps_ref[z + 1, x + 1, :, 2 * channels :] = high.astype(bf16)
+        return carry
+
+    lax.fori_loop(0, slabs, fill, 0)
+
+    half_zeros = jnp.zeros((half_rows, wide), bf16)
+    for x in range(extent_x + 1):
+        strided_ref[0, x] = half_zeros
+
+    def front(z, carry):
+        total = jnp.zeros((extent_x * rows, channels), f32)
+        for kz in range(3):
+            for kx in range(3):
+                window = taps_ref[z + kz, kx : kx + extent_x].reshape(extent_x * rows, wide)
+                kernel = front_ref[3 * (3 * kz + kx) : 3 * (3 * kz + kx) + 3].reshape(wide, channels)
+                total += jnp.dot(window, kernel, preferred_element_type=f32)
+        logistic = 1.0 / (1.0 + jnp.exp(-total))
+        act = (total * logistic).astype(bf16).astype(f32)
+        slope = logistic * (1.0 + total * (1.0 - logistic))
+        act_ref[z] = act.reshape(extent_x, rows, channels)
+        slope_ref[z] = slope.reshape(extent_x, rows, channels)
+        strided_ref[z + 1, 0] = half_zeros
+        for x in range(extent_x):
+            even = act_ref[z, x, pl.ds(0, half_rows, stride=2), :]
+            odd = act_ref[z, x, pl.ds(1, half_rows, stride=2), :]
+            low = jnp.where(half_first, 0.0, pltpu.roll(odd, 1, 0))
+            strided_ref[z + 1, x + 1, :, :channels] = low.astype(bf16)
+            strided_ref[z + 1, x + 1, :, channels : 2 * channels] = even.astype(bf16)
+            strided_ref[z + 1, x + 1, :, 2 * channels :] = odd.astype(bf16)
+        return carry
+
+    lax.fori_loop(0, depth, front, 0)
+
+    def strided_window(kz, kx):
+        return jnp.concatenate(
+            [strided_ref[kz + 2 * z, kx + 2 * x] for z in range(half_z) for x in range(half_x)], axis=0
+        )
+
+    def stride_kernel(kz, kx):
+        start = 3 * (3 * kz + kx)
+        return stride_ref[start : start + 3].reshape(wide, stride_ref.shape[-1])
+
+    pre = None
+    for kz in range(3):
+        for kx in range(3):
+            term = jnp.dot(strided_window(kz, kx), stride_kernel(kz, kx), preferred_element_type=f32)
+            pre = term if pre is None else pre + term
+    logistic = 1.0 / (1.0 + jnp.exp(-pre))
+    planes = half_z * half_x
+    features = pre.shape[-1]
+    summed = jnp.sum((pre * logistic).reshape(planes, half_rows, features), axis=0)
+    owner = lax.broadcasted_iota(jnp.int32, (samples, half_rows), 1)
+    sample = lax.broadcasted_iota(jnp.int32, (samples, half_rows), 0)
+    member = ((owner >= sample * half_y) & (owner < (sample + 1) * half_y)).astype(f32)
+    pooled = jnp.dot(member, summed, precision=highest, preferred_element_type=f32) / cells
+    hidden = hidden_ref[...]
+    output = output_ref[...]
+
+    def contract(left, right, dims):
+        return lax.dot_general(left, right, (dims, ((), ())), precision=highest, preferred_element_type=f32)
+
+    hidden_pre = contract(pooled, hidden, ((1,), (0,)))
+    hidden_logistic = 1.0 / (1.0 + jnp.exp(-hidden_pre))
+    hidden_act = hidden_pre * hidden_logistic
+    residual = contract(hidden_act, output, ((1,), (0,))) - targets_ref[...]
+    loss_ref[...] = jnp.sum(residual * residual, keepdims=True) / (samples * output.shape[-1])
+    grad_output_ref[...] = contract(hidden_act, residual, ((0,), (0,)))
+    hidden_slope = hidden_logistic * (1.0 + hidden_pre * (1.0 - hidden_logistic))
+    grad_hidden_pre = contract(residual, output, ((1,), (1,))) * hidden_slope
+    share = features // 2
+    pooled_own = jnp.where(lax.axis_index("chan") == 0, pooled[:, :share], pooled[:, share:])
+    grad_hidden_ref[...] = contract(pooled_own, grad_hidden_pre, ((0,), (0,)))
+    grad_pooled = contract(grad_hidden_pre, hidden, ((1,), (1,)))
+    grad_rows = contract(member, grad_pooled, ((0,), (0,))) / cells
+    slope = logistic * (1.0 + pre * (1.0 - logistic))
+    grad_pre = (slope.reshape(planes, half_rows, features) * grad_rows[None]).astype(bf16)
+    grad_pre = grad_pre.reshape(planes * half_rows, features)
+
+    for kz in range(3):
+        for kx in range(3):
+            start = 3 * (3 * kz + kx)
+            spread = lax.dot_general(
+                grad_pre, stride_kernel(kz, kx), (((1,), (1,)), ((), ())), preferred_element_type=f32
+            )
+            spread_ref[3 * kz + kx] = spread.reshape(planes, half_rows, wide)
+            kernel = lax.dot_general(
+                strided_window(kz, kx), grad_pre, (((0,), (0,)), ((), ())), preferred_element_type=f32
+            )
+            for ky in range(3):
+                grad_stride_ref[start + ky] = kernel[ky * channels : ky * channels + inner]
+
+    def sources(cell, half):
+        if cell % 2 == 0:
+            return [(1, cell // 2)]
+        found = [(2, cell // 2)]
+        if cell // 2 + 1 < half:
+            found.append((0, cell // 2 + 1))
+        return found
+
+    for z in range(depth):
+        for x in range(extent_x):
+            total = None
+            for kz, from_z in sources(z, half_z):
+                for kx, from_x in sources(x, half_x):
+                    block = spread_ref[3 * kz + kx, from_z * half_x + from_x]
+                    total = block if total is None else total + block
+            even = total[:, channels : 2 * channels]
+            up = jnp.where(half_last, 0.0, pltpu.roll(total[:, :channels], half_rows - 1, 0))
+            odd = total[:, 2 * channels :] + up
+            for start, grad in ((0, even), (1, odd)):
+                grad = grad.astype(bf16).astype(f32)
+                place = pl.ds(start, half_rows, stride=2)
+                grad_pre_ref[z, x, place, :] = grad * slope_ref[z, x, place, :]
+
+    grads = grad_pre_ref[...].reshape(depth * extent_x * rows, channels).astype(bf16)
+    grads = jnp.transpose(grads)[:inner]
+    for kz in range(3):
+        for kx in range(3):
+            window = taps_ref[kz : kz + depth, kx : kx + extent_x]
+            window = window.reshape(depth * extent_x * rows, wide)
+            turned = jnp.dot(grads, window, preferred_element_type=f32)
+            for ky in range(3):
+                grad_front_ref[3 * (3 * kz + kx) + ky] = jnp.transpose(
+                    turned[:, ky * channels : (ky + 1) * channels]
+                )
+
+
+def whole_batch(shape, features, gathered, targets, front_own, front_other, stride_all, hidden_all, output_weight):
+    slabs, batches, leading, thick, extent_x, extent_y, channels, inner = shape
+    samples, depth = batches * leading, slabs * thick
+    rows = samples * extent_y
+    half_rows = rows // 2
+    planes = depth * extent_x // 4
+    f32, bf16 = jnp.float32, jnp.bfloat16
+    outputs = output_weight.shape[-1]
+    hid = hidden_all.shape[-1]
+    vmem = pl.BlockSpec(memory_space=pltpu.VMEM)
+    return pl.pallas_call(
+        functools.partial(whole_kernel, shape),
+        out_shape=(
+            jax.ShapeDtypeStruct((27, channels, inner), f32),
+            jax.ShapeDtypeStruct((27, inner, features), f32),
+            jax.ShapeDtypeStruct((features // 2, hid), f32),
+            jax.ShapeDtypeStruct((hid, outputs), f32),
+            jax.ShapeDtypeStruct((1, 1), f32),
+        ),
+        in_specs=[vmem] * 7,
+        out_specs=[vmem] * 5,
+        scratch_shapes=[
+            pltpu.VMEM((depth + 2, extent_x + 2, rows, 3 * channels), bf16),
+            pltpu.VMEM((27, channels, channels), bf16),
+            pltpu.VMEM((depth, extent_x, rows, channels), f32),
+            pltpu.VMEM((depth, extent_x, rows, channels), f32),
+            pltpu.VMEM((depth + 1, extent_x + 1, half_rows, 3 * channels), bf16),
+            pltpu.VMEM((9, planes, half_rows, 3 * channels), f32),
+            pltpu.VMEM((depth, extent_x, rows, channels), f32),
+        ],
+        compiler_params=pltpu.CompilerParams(vmem_limit_bytes=48 << 20),
+    )(gathered, targets, front_own, front_other, stride_all, hidden_all, output_weight)
+
+
+def gather_inputs(volume, targets, front_weight, stride_weight, hidden_weight):
+    inner = front_weight.shape[-1]
+    channels = volume.shape[-1]
+    swap = [(0, 1), (1, 0)]
+    gathered = lax.all_gather(volume, ("batch", "slab"))
+    targets = lax.all_gather(targets, "batch", tiled=True)
+    front_own = front_weight.reshape(27, channels, inner)
+    stride_own = stride_weight.reshape(27, inner, -1)
+    front_other = lax.ppermute(front_own, "chan", swap)
+    stride_other = lax.ppermute(stride_own, "chan", swap)
+    stride_all = jnp.concatenate([stride_own, stride_other], axis=1)
+    hidden_all = lax.all_gather(hidden_weight, "chan", tiled=True)
+    return gathered, targets, front_own, front_other, stride_all, hidden_all
+
+
+def body(volume, targets, front_weight, stride_weight, hidden_weight, output_weight):
+    slabs = lax.axis_size("slab")
+    batches = lax.axis_size("batch")
+    if volume.size * 2 * slabs * batches > GATHER_LIMIT:
+        return split_body(volume, targets, front_weight, stride_weight, hidden_weight, output_weight)
+    inner = front_weight.shape[-1]
+    channels = volume.shape[-1]
+    features = stride_weight.shape[-1]
+    shape = (slabs, batches) + volume.shape + (inner,)
+    gathered = gather_inputs(volume, targets, front_weight, stride_weight, hidden_weight)
+    grad_front, grad_stride, grad_hidden, grad_output, loss = whole_batch(
+        shape, features, *gathered, output_weight
+    )
+    return (
+        grad_front.reshape(3, 3, 3, channels, inner),
+        grad_stride.reshape(3, 3, 3, inner, features),
+        grad_hidden,
+        grad_output,
+        loss.reshape(1),
+    )
+
+
 def solution(mesh):
     in_specs = (
         P(("groups", "batch"), "slab", None, None, None),

time: 214 us -> 65.5 us (0.31)
  waiting for transfers between devices: 112 us -> 0.01 us
  matrix products: 23.2 us -> 0 us
  between operations: 16.7 us -> 0.69 us
  Pallas kernels: 0 us -> 13.3 us
  starting transfers between devices: 11.2 us -> 0.6 us
  blocking collectives: 33.9 us -> 40.9 us
  local copies, waits for them, and re-layouts: 13.5 us -> 8.47 us
    psum x1 -> x0, waiting for transfers between devices: 96.9 us -> none  [body(): lax.psum((grad_front, grad_stride, grad_hidden, grad_output, squared), ('...]
    all_gather x1 -> x3, blocking collectives: 1.82 us -> 40.9 us  [the longest x1 33.4 us: gather_inputs(): gathered = lax.all_gather(volume, ('batch', 'slab'))]
    dot_general x139 -> x0, matrix products: 23.2 us -> none  [the longest x54 10.2 us: kernel_grad(): lax.dot_general(flat_tap, flat_grad, (((0,), (0,)), ((), ())), preferred_...]
    psum x2 -> x0, blocking collectives: 22.8 us -> none  [the longest x1 20.3 us: body(): lax.psum((grad_front, grad_stride, grad_hidden, grad_output, squared), ('...]
    pallas_call x0 -> x1, Pallas kernels: none -> 13.3 us  [whole_batch(): pl.pallas_call(functools.partial(whole_kernel, shape), out_shape=(jax.Sha...]
    all_to_all x1 -> x0, blocking collectives: 9.32 us -> none  [body(): lax.all_to_all(merged, 'slab', split_axis=0, concat_axis=1, tiled=True)]
    unnamed x3 -> x0, waiting for transfers between devices: 6.09 us -> none
    ppermute x2, starting transfers between devices: 6.34 us -> 0.6 us  [the longest x1 0.52 us: gather_inputs(): stride_other = lax.ppermute(stride_own, 'chan', swap)]
  transfers between devices with their start and end apart: 5 -> 2, of which waited for: 5 -> 0; matrix products, arithmetic and copies ran while one was open for 0% -> 6% of each run, Pallas kernels for 0% -> 0%
where the time goes in v1:
time: 65.5 us; the launch traced here: 65.2 us
  blocking collectives  40.9 us (62%)
  Pallas kernels  13.3 us (20%)
  local copies, waits for them, and re-layouts  8.47 us (13%)
  other arithmetic  1.31 us (2%)
  between operations  0.69 us (1%)
    all_gather x1, blocking collectives, gather_inputs(): gathered = lax.all_gather(volume, ('batch', 'slab'))  33.4 us
    pallas_call x1, Pallas kernels, whole_batch(): pl.pallas_call(functools.partial(whole_kernel, shape), out_shape=(jax.Sha...  13.3 us
    unnamed x8, local copies, waits for them, and re-layouts  7.03 us
    all_gather x1, blocking collectives, gather_inputs(): targets = lax.all_gather(targets, 'batch', tiled=True)  5.4 us
    all_gather x1, blocking collectives, gather_inputs(): hidden_all = lax.all_gather(hidden_weight, 'chan', tiled=True)  2.11 us
    ppermute x1, local copies, waits for them, and re-layouts, gather_inputs(): front_other = lax.ppermute(front_own, 'chan', swap)  1.44 us
    concatenate x1, other arithmetic, gather_inputs(): stride_all = jnp.concatenate([stride_own, stride_other], axis=1)  1.31 us
  transfers between devices with their start and end apart: 2, of which 0 were waited for; matrix products, arithmetic and copies ran while one was open for 6% of the time, Pallas kernels for 0%

profile of v1, /device:TPU:0, one launch (start us, length us, event | category | flops | bytes accessed | tf_op | source)
XLA Modules:
  0.0 65.2 jit_solution(6328698385377770101)
XLA Ops:
  0.6 0.0 copy-start.1
  0.6 0.5 collective-permute-start.1
  1.2 0.1 collective-permute-start
  1.2 5.4 %all-gather.1 = f32[2,4,4]{2,1,0:T(4,128)S(1)} all-gather(f32[1,4,4]{2,1,0:T(4,128)} %bitcast.16), channel_id=1, replica_groups=mesh['groups'=2,'slab'=4,'batch'=2,'chan'=2] {'batch'}, dimensions={0}, use_global_device_ids=true | all-gather | bytes 192 | tf_op jit(solution)/shard_map/all_gather | solution.py:403
  6.6 1.4 %copy.18 = bf16[3,3,3,128,64]{4,3,2,1,0:T(8,128)(2,1)S(1)} copy(bf16[3,3,3,128,64]{3,4,2,1,0:T(8,128)(2,1)} %param.8) | data formatting | bytes 884736 | tf_op args[2]
  8.1 0.8 %copy.22.output_ref = f32[128,4]{1,0:T(8,128)S(1)} copy(f32[128,4]{0,1:T(4,128)} %param.11) | data formatting | bytes 4096 | tf_op args[5]
  8.9 2.1 %all_gather.15.hidden_ref = f32[256,128]{1,0:T(8,128)S(1)} all-gather(f32[128,128]{1,0:T(8,128)} %param.10), channel_id=1, replica_groups=mesh['groups'=2,'slab'=4,'batch'=2,'chan'=2] {'chan'}, dimensions={0}, use_global_device_ids=true | all-gather | bytes 196608 | tf_op jit(solution)/shard_map/all_gather | solution.py:409
  11.0 33.4 %all-gather = bf16[32,2,4,8,128]{4,3,2,1,0:T(8,128)(2,1)S(1)} all-gather(bf16[4,2,4,8,128]{4,3,2,1,0:T(8,128)(2,1)} %param.6), channel_id=2, replica_groups=mesh['groups'=2,'slab'=4,'batch'=2,'chan'=2] {'batch','slab'}, dimensions={0}, use_global_device_ids=true | all-gather | bytes 589824 | tf_op jit(solution)/shard_map/all_gather | solution.py:402
  44.3 0.0 collective-permute-done
  44.3 1.4 %copy.21.front_other_ref = bf16[27,128,64]{2,1,0:T(8,128)(2,1)S(1)} copy(bf16[27,128,64]{1,2,0:T(8,128)(2,1)} %collective-permute-done) | data formatting | bytes 884736 | tf_op jit(solution)/shard_map/ppermute | solution.py:406
  45.8 0.0 collective-permute-done.1
  45.8 0.0 copy-done.1
  45.8 1.3 %pad_maximum_fusion.stride_ref = bf16[27,128,256]{2,1,0:T(8,128)(2,1)S(1)} fusion(bf16[27,64,256]{2,1,0:T(8,128)(2,1)} %collective-permute-done.1, bf16[27,64,256]{2,1,0:T(8,128)(2,1)S(1)} %bitcast.14), kind=kLoop, calls=%fused_computation | loop fusion | flops 3538944 | bytes 3538944 | tf_op jit(solution)/shard_map/concatenate | solution.py:408
  47.1 13.3 %shard_map.101 = (f32[27,128,64]{2,1,0:T(8,128)S(1)}, f32[27,64,256]{2,1,0:T(8,128)}, f32[128,128]{1,0:T(8,128)}, f32[128,4]{1,0:T(8,128)S(1)}, f32[1,1]{1,0:T(1,128)}) custom-call(bf16[8,4,2,4,8,128]{5,4,3,2,1,0:T(8,128)(2,1)S(1)} %bitcast.10, f32[8,4]{1,0:T(8,128)S(1)} %bitcast.12, bf16[27,128,64]{2,1,0:T(8,128)(2,1)S(1)} %bitcast.9, ...), custom_call_target="tpu_custom_call" | custom-call | tf_op jit(solution)/shard_map/pallas_call | solution.py:374
  60.4 0.0 copy-start
  60.4 1.2 %copy-done = f32[27,128,64]{2,1,0:T(8,128)} copy-done((f32[27,128,64]{2,1,0:T(8,128)}, f32[27,128,64]{2,1,0:T(8,128)S(1)}, u32[]{:S(2)}) %copy-start) | copy-done | bytes 884760
  61.7 2.9 %copy.23 = f32[3,3,3,128,64]{3,4,2,1,0:T(8,128)} copy(f32[3,3,3,128,64]{4,3,2,1,0:T(8,128)} %bitcast.11) | data formatting | bytes 1769472
  64.6 0.7 copy.24
Async XLA Ops:
  0.6 45.2 %copy-start.1 = (bf16[3,3,3,64,256]{4,3,2,1,0:T(8,128)(2,1)S(1)}, bf16[3,3,3,64,256]{4,3,2,1,0:T(8,128)(2,1)}, u32[]{:S(2)}) copy-start(bf16[3,3,3,64,256]{4,3,2,1,0:T(8,128)(2,1)} %param.9) | copy-start | bytes 2654212
  0.6 45.1 %collective-permute-start.1 = (bf16[27,64,256]{2,1,0:T(8,128)(2,1)}, bf16[27,64,256]{2,1,0:T(8,128)(2,1)}, u32[]{:S(2)}, u32[]{:S(2)}) collective-permute-start(bf16[27,64,256]{2,1,0:T(8,128)(2,1)} %bitcast.13), channel_id=1, source_target_pairs={{0,1},{1,0},{2,3},{3,2},{4,5},{5,4},{6,7},{7,6},{8,9},{9,8},{10,11... | collective-permute-start | bytes 2654216 | tf_op jit(solution)/shard_map/ppermute | solution.py:407
  1.2 43.2 %collective-permute-start = (bf16[27,128,64]{1,2,0:T(8,128)(2,1)}, bf16[27,128,64]{1,2,0:T(8,128)(2,1)}, u32[]{:S(2)}, u32[]{:S(2)}) collective-permute-start(bf16[27,128,64]{1,2,0:T(8,128)(2,1)} %bitcast.15), channel_id=1, source_target_pairs={{0,1},{1,0},{2,3},{3,2},{4,5},{5,4},{6,7},{7,6},{8,9},{9,8},{10,11... | collective-permute-start | bytes 1327112 | tf_op jit(solution)/shard_map/ppermute | solution.py:406
  60.4 1.3 %copy-start = (f32[27,128,64]{2,1,0:T(8,128)}, f32[27,128,64]{2,1,0:T(8,128)S(1)}, u32[]{:S(2)}) copy-start(f32[27,128,64]{2,1,0:T(8,128)S(1)} %get-tuple-element.10) | copy-start | bytes 2654212

commit v2 on v1

--- a/solution.py
+++ b/solution.py
@@ -186,9 +186,10 @@
 
 def whole_kernel(
     shape,
-    volume_ref, targets_ref, front_own_ref, front_other_ref, stride_ref, hidden_ref, output_ref,
+    volume_ref, targets_ref, front_turned_ref, stride_ref, hidden_ref, output_ref,
     grad_front_ref, grad_stride_ref, grad_hidden_ref, grad_output_ref, loss_ref,
     taps_ref, front_ref, act_ref, slope_ref, strided_ref, spread_ref, grad_pre_ref,
+    front_out_ref, stride_out_ref, front_sem, stride_sem,
 ):
     slabs, batches, leading, thick, extent_x, extent_y, channels, inner = shape
     f32, bf16 = jnp.float32, jnp.bfloat16
@@ -202,8 +203,8 @@
     wide = 3 * channels
     local_rows = leading * extent_y
 
-    front_ref[:, :, :inner] = front_own_ref[...]
-    front_ref[:, :, inner:] = front_other_ref[...]
+    for tap in range(27):
+        front_ref[tap] = jnp.transpose(front_turned_ref[tap])
 
     zeros = jnp.zeros((rows, wide), bf16)
     for x in range(extent_x + 2):
@@ -298,11 +299,11 @@
     hidden_pre = contract(pooled, hidden, ((1,), (0,)))
     hidden_logistic = 1.0 / (1.0 + jnp.exp(-hidden_pre))
     hidden_act = hidden_pre * hidden_logistic
-    residual = contract(hidden_act, output, ((1,), (0,))) - targets_ref[...]
-    loss_ref[...] = jnp.sum(residual * residual, keepdims=True) / (samples * output.shape[-1])
-    grad_output_ref[...] = contract(hidden_act, residual, ((0,), (0,)))
+    residual = contract(hidden_act, output, ((1,), (1,))) - targets_ref[...]
+    loss_ref[...] = jnp.sum(residual * residual, keepdims=True) / (samples * output.shape[0])
+    grad_output_ref[...] = contract(residual, hidden_act, ((0,), (0,)))
     hidden_slope = hidden_logistic * (1.0 + hidden_pre * (1.0 - hidden_logistic))
-    grad_hidden_pre = contract(residual, output, ((1,), (1,))) * hidden_slope
+    grad_hidden_pre = contract(residual, output, ((1,), (0,))) * hidden_slope
     share = features // 2
     pooled_own = jnp.where(lax.axis_index("chan") == 0, pooled[:, :share], pooled[:, share:])
     grad_hidden_ref[...] = contract(pooled_own, grad_hidden_pre, ((0,), (0,)))
@@ -311,6 +312,10 @@
     slope = logistic * (1.0 + pre * (1.0 - logistic))
     grad_pre = (slope.reshape(planes, half_rows, features) * grad_rows[None]).astype(bf16)
     grad_pre = grad_pre.reshape(planes * half_rows, features)
+
+    def send_out(source, target, sems, group):
+        place = pl.ds(3 * group, 3)
+        return pltpu.make_async_copy(source.at[place], target.at[place], sems.at[group])
 
     for kz in range(3):
         for kx in range(3):
@@ -323,7 +328,8 @@
                 strided_window(kz, kx), grad_pre, (((0,), (0,)), ((), ())), preferred_element_type=f32
             )
             for ky in range(3):
-                grad_stride_ref[start + ky] = kernel[ky * channels : ky * channels + inner]
+                stride_out_ref[start + ky] = kernel[ky * channels : ky * channels + inner]
+            send_out(stride_out_ref, grad_stride_ref, stride_sem, 3 * kz + kx).start()
 
     def sources(cell, half):
         if cell % 2 == 0:
@@ -356,32 +362,34 @@
             window = window.reshape(depth * extent_x * rows, wide)
             turned = jnp.dot(grads, window, preferred_element_type=f32)
             for ky in range(3):
-                grad_front_ref[3 * (3 * kz + kx) + ky] = jnp.transpose(
-                    turned[:, ky * channels : (ky + 1) * channels]
-                )
-
-
-def whole_batch(shape, features, gathered, targets, front_own, front_other, stride_all, hidden_all, output_weight):
+                front_out_ref[3 * (3 * kz + kx) + ky] = turned[:, ky * channels : (ky + 1) * channels]
+            send_out(front_out_ref, grad_front_ref, front_sem, 3 * kz + kx).start()
+    for group in range(9):
+        send_out(stride_out_ref, grad_stride_ref, stride_sem, group).wait()
+        send_out(front_out_ref, grad_front_ref, front_sem, group).wait()
+
+
+def whole_batch(shape, features, gathered, targets, front_all, stride_all, hidden_all, output_turned):
     slabs, batches, leading, thick, extent_x, extent_y, channels, inner = shape
     samples, depth = batches * leading, slabs * thick
     rows = samples * extent_y
     half_rows = rows // 2
     planes = depth * extent_x // 4
     f32, bf16 = jnp.float32, jnp.bfloat16
-    outputs = output_weight.shape[-1]
-    hid = hidden_all.shape[-1]
+    outputs, hid = output_turned.shape
     vmem = pl.BlockSpec(memory_space=pltpu.VMEM)
+    anywhere = pl.BlockSpec(memory_space=pl.ANY)
     return pl.pallas_call(
         functools.partial(whole_kernel, shape),
         out_shape=(
-            jax.ShapeDtypeStruct((27, channels, inner), f32),
+            jax.ShapeDtypeStruct((27, inner, channels), f32),
             jax.ShapeDtypeStruct((27, inner, features), f32),
             jax.ShapeDtypeStruct((features // 2, hid), f32),
-            jax.ShapeDtypeStruct((hid, outputs), f32),
+            jax.ShapeDtypeStruct((outputs, hid), f32),
             jax.ShapeDtypeStruct((1, 1), f32),
         ),
-        in_specs=[vmem] * 7,
-        out_specs=[vmem] * 5,
+        in_specs=[vmem] * 6,
+        out_specs=[anywhere] * 2 + [vmem] * 3,
         scratch_shapes=[
             pltpu.VMEM((depth + 2, extent_x + 2, rows, 3 * channels), bf16),
             pltpu.VMEM((27, channels, channels), bf16),
@@ -390,44 +398,169 @@
             pltpu.VMEM((depth + 1, extent_x + 1, half_rows, 3 * channels), bf16),
             pltpu.VMEM((9, planes, half_rows, 3 * channels), f32),
             pltpu.VMEM((depth, extent_x, rows, channels), f32),
+            pltpu.VMEM((27, inner, channels), f32),
+            pltpu.VMEM((27, inner, features), f32),
+            pltpu.SemaphoreType.DMA((9,)),
+            pltpu.SemaphoreType.DMA((9,)),
         ],
-        compiler_params=pltpu.CompilerParams(vmem_limit_bytes=48 << 20),
-    )(gathered, targets, front_own, front_other, stride_all, hidden_all, output_weight)
-
-
-def gather_inputs(volume, targets, front_weight, stride_weight, hidden_weight):
-    inner = front_weight.shape[-1]
-    channels = volume.shape[-1]
-    swap = [(0, 1), (1, 0)]
-    gathered = lax.all_gather(volume, ("batch", "slab"))
-    targets = lax.all_gather(targets, "batch", tiled=True)
-    front_own = front_weight.reshape(27, channels, inner)
-    stride_own = stride_weight.reshape(27, inner, -1)
-    front_other = lax.ppermute(front_own, "chan", swap)
-    stride_other = lax.ppermute(stride_own, "chan", swap)
-    stride_all = jnp.concatenate([stride_own, stride_other], axis=1)
-    hidden_all = lax.all_gather(hidden_weight, "chan", tiled=True)
-    return gathered, targets, front_own, front_other, stride_all, hidden_all
+        compiler_params=pltpu.CompilerParams(vmem_limit_bytes=40 << 20),
+    )(gathered, targets, front_all, stride_all, hidden_all, output_turned)
+
+
+def gather_kernel(
+    slabs, batches,
+    volume_ref, targets_ref, front_ref, stride_ref, hidden_ref,
+    gathered_ref, targets_all_ref, front_all_ref, stride_all_ref, hidden_all_ref,
+    local_sem, slab_sem, batch_sem, piece_sem, pair_send_sem, pair_sem,
+    target_send_sem, target_sem, weight_send_sem, weight_sem,
+):
+    slab, batch, chan = lax.axis_index("slab"), lax.axis_index("batch"), lax.axis_index("chan")
+    sibling = {"chan": 1 - chan}
+    half = volume_ref.shape[0] // 2
+    inner = front_ref.shape[1]
+    share = hidden_ref.shape[0]
+
+    def remote(source, target, send_sem, recv_sem, device):
+        return pltpu.make_async_remote_copy(
+            src_ref=source, dst_ref=target, send_sem=send_sem, recv_sem=recv_sem,
+            device_id=device, device_id_type=pl.DeviceIdType.MESH,
+        )
+
+    slab_steps = range(1, slabs)
+    batch_steps = range(1, batches)
+    to_slab = [{"slab": lax.rem(slab + step, slabs)} for step in slab_steps]
+    to_batch = [{"batch": lax.rem(batch + step, batches)} for step in batch_steps]
+    from_slab = [lax.rem(slab + slabs - step, slabs) for step in slab_steps]
+    from_batch = [lax.rem(batch + batches - step, batches) for step in batch_steps]
+
+    barrier = pltpu.get_barrier_semaphore()
+    neighbours = to_slab + to_batch + [sibling]
+    for device in neighbours:
+        pl.semaphore_signal(barrier, inc=1, device_id=device, device_id_type=pl.DeviceIdType.MESH)
+    pl.semaphore_wait(barrier, len(neighbours))
+
+    def part(piece, side):
+        return gathered_ref.at[piece, pl.ds(side * half, half)]
+
+    mine = batch * slabs + slab
+    own = volume_ref.at[pl.ds(chan * half, half)]
+    sends = []
+
+    def send(copy):
+        copy.start()
+        sends.append(copy)
+
+    for i, device in enumerate(to_slab):
+        send(remote(own, part(mine, chan), slab_sem.at[i], piece_sem.at[mine], device))
+    for i, device in enumerate(to_batch):
+        send(remote(own, part(mine, chan), batch_sem.at[0, i], piece_sem.at[mine], device))
+        send(remote(targets_ref, targets_all_ref.at[batch], target_send_sem.at[i], target_sem.at[batch], device))
+    weights = [
+        remote(front_ref, front_all_ref.at[:, pl.ds(inner, inner)], weight_send_sem.at[0], weight_sem.at[0], sibling),
+        remote(stride_ref, stride_all_ref.at[:, pl.ds(inner, inner)], weight_send_sem.at[1], weight_sem.at[1], sibling),
+        remote(hidden_ref, hidden_all_ref.at[pl.ds(chan * share, share)], weight_send_sem.at[2], weight_sem.at[2], sibling),
+    ]
+    for copy in weights:
+        send(copy)
+    local = [
+        pltpu.make_async_copy(volume_ref, gathered_ref.at[mine], local_sem.at[0]),
+        pltpu.make_async_copy(targets_ref, targets_all_ref.at[batch], local_sem.at[1]),
+        pltpu.make_async_copy(front_ref, front_all_ref.at[:, pl.ds(0, inner)], local_sem.at[2]),
+        pltpu.make_async_copy(stride_ref, stride_all_ref.at[:, pl.ds(0, inner)], local_sem.at[3]),
+        pltpu.make_async_copy(hidden_ref, hidden_all_ref.at[pl.ds(chan * share, share)], local_sem.at[4]),
+    ]
+    for copy in local:
+        copy.start()
+
+    def arrived(piece, side, sem, device):
+        remote(part(piece, side), part(piece, side), slab_sem.at[0], sem.at[piece], device).wait_recv()
+
+    def pass_on(slot, piece):
+        send(remote(part(piece, chan), part(piece, chan), pair_send_sem.at[slot], pair_sem.at[piece], sibling))
+
+    slot = 0
+    for j, source in enumerate(from_slab):
+        piece = batch * slabs + source
+        arrived(piece, chan, piece_sem, sibling)
+        for i, device in enumerate(to_batch):
+            send(remote(part(piece, chan), part(piece, chan), batch_sem.at[j + 1, i], piece_sem.at[piece], device))
+        pass_on(slot, piece)
+        slot += 1
+    for source in from_batch:
+        for slab_source in [slab] + from_slab:
+            piece = source * slabs + slab_source
+            arrived(piece, chan, piece_sem, sibling)
+            pass_on(slot, piece)
+            slot += 1
+        remote(
+            targets_ref, targets_all_ref.at[source], target_send_sem.at[0], target_sem.at[source], sibling
+        ).wait_recv()
+    for source in [batch] + from_batch:
+        for slab_source in [slab] + from_slab:
+            if source is batch and slab_source is slab:
+                continue
+            arrived(source * slabs + slab_source, 1 - chan, pair_sem, sibling)
+    for copy in weights:
+        copy.wait_recv()
+    for copy in local:
+        copy.wait()
+    for copy in sends:
+        copy.wait_send()
+
+
+def gather_inputs(volume, targets, front_turned, stride_own, hidden_weight):
+    slabs, batches = lax.axis_size("slab"), lax.axis_size("batch")
+    pieces = slabs * batches
+    vmem = pl.BlockSpec(memory_space=pltpu.VMEM)
+    hbm = pl.BlockSpec(memory_space=pltpu.HBM)
+    taps, inner, channels = front_turned.shape
+    features = stride_own.shape[-1]
+    share, hid = hidden_weight.shape
+    dma = pltpu.SemaphoreType.DMA
+    return pl.pallas_call(
+        functools.partial(gather_kernel, slabs, batches),
+        out_shape=(
+            jax.ShapeDtypeStruct((pieces,) + volume.shape, volume.dtype),
+            jax.ShapeDtypeStruct((batches,) + targets.shape, targets.dtype),
+            jax.ShapeDtypeStruct((taps, 2 * inner, channels), front_turned.dtype),
+            jax.ShapeDtypeStruct((taps, 2 * inner, features), stride_own.dtype),
+            jax.ShapeDtypeStruct((2 * share, hid), hidden_weight.dtype),
+        ),
+        in_specs=[hbm] * 5,
+        out_specs=[vmem] * 5,
+        scratch_shapes=[
+            dma((5,)), dma((slabs,)), dma((slabs, batches)), dma((pieces,)), dma((pieces,)), dma((pieces,)),
+            dma((batches,)), dma((batches,)), dma((3,)), dma((3,)),
+        ],
+        compiler_params=pltpu.CompilerParams(
+            collective_id=0, has_side_effects=True, vmem_limit_bytes=16 << 20
+        ),
+    )(volume, targets, front_turned, stride_own, hidden_weight)
 
 
 def body(volume, targets, front_weight, stride_weight, hidden_weight, output_weight):
     slabs = lax.axis_size("slab")
     batches = lax.axis_size("batch")
-    if volume.size * 2 * slabs * batches > GATHER_LIMIT:
+    if volume.size * 2 * slabs * batches > GATHER_LIMIT or volume.shape[0] % 2:
         return split_body(volume, targets, front_weight, stride_weight, hidden_weight, output_weight)
     inner = front_weight.shape[-1]
     channels = volume.shape[-1]
     features = stride_weight.shape[-1]
     shape = (slabs, batches) + volume.shape + (inner,)
-    gathered = gather_inputs(volume, targets, front_weight, stride_weight, hidden_weight)
+    front_turned = jnp.swapaxes(front_weight.reshape(27, channels, inner), 1, 2)
+    stride_own = stride_weight.reshape(27, inner, features)
+    gathered, targets, front_all, stride_all, hidden_all = gather_inputs(
+        volume, targets, front_turned, stride_own, hidden_weight
+    )
     grad_front, grad_stride, grad_hidden, grad_output, loss = whole_batch(
-        shape, features, *gathered, output_weight
+        shape, features, gathered, targets.reshape(-1, targets.shape[-1]),
+        front_all, stride_all, hidden_all, output_weight.T,
     )
     return (
-        grad_front.reshape(3, 3, 3, channels, inner),
+        jnp.swapaxes(grad_front, 1, 2).reshape(3, 3, 3, channels, inner),
         grad_stride.reshape(3, 3, 3, inner, features),
         grad_hidden,
-        grad_output,
+        grad_output.T,
         loss.reshape(1),
     )
 

time: 65.5 us -> 34.1 us (0.52)
  blocking collectives: 40.9 us -> 0 us
  Pallas kernels: 13.3 us -> 27.9 us
  local copies, waits for them, and re-layouts: 8.47 us -> 5.21 us
  other arithmetic: 1.31 us -> 0 us
    all_gather x3 -> x0, blocking collectives: 40.9 us -> none  [the longest x1 33.4 us: gather_inputs(): gathered = lax.all_gather(volume, ('batch', 'slab'))]
    pallas_call x0 -> x1, Pallas kernels: none -> 13.5 us  [gather_inputs(): pl.pallas_call(functools.partial(gather_kernel, slabs, batches), out_shap...]
    unnamed x8 -> x12, local copies, waits for them, and re-layouts: 7.03 us -> 5.21 us
    ppermute x1 -> x0, local copies, waits for them, and re-layouts: 1.44 us -> none  [gather_inputs(): front_other = lax.ppermute(front_own, 'chan', swap)]
    concatenate x1 -> x0, other arithmetic: 1.31 us -> none  [gather_inputs(): stride_all = jnp.concatenate([stride_own, stride_other], axis=1)]
    pallas_call x1, Pallas kernels: 13.3 us -> 14.3 us  [whole_batch(): pl.pallas_call(functools.partial(whole_kernel, shape), out_shape=(jax.Sha...]
  transfers between devices with their start and end apart: 2 -> 0, of which waited for: 0 -> 0; matrix products, arithmetic and copies ran while one was open for 6% -> 0% of each run, Pallas kernels for 0% -> 0%
where the time goes in v2:
time: 34.1 us; the launch traced here: 33.7 us
  Pallas kernels  27.9 us (82%)
  local copies, waits for them, and re-layouts  5.21 us (15%)
  between operations  0.66 us (2%)
    pallas_call x1, Pallas kernels, whole_batch(): pl.pallas_call(functools.partial(whole_kernel, shape), out_shape=(jax.Sha...  14.3 us
    pallas_call x1, Pallas kernels, gather_inputs(): pl.pallas_call(functools.partial(gather_kernel, slabs, batches), out_shap...  13.5 us
    unnamed x12, local copies, waits for them, and re-layouts  5.21 us

profile of v2, /device:TPU:0, one launch (start us, length us, event | category | flops | bytes accessed | tf_op | source)
XLA Modules:
  0.0 33.7 jit_solution(8854152237056497491)
XLA Ops:
  0.6 0.0 copy-start
  0.6 1.2 %copy-done = bf16[3,3,3,64,256]{4,3,2,1,0:T(8,128)(2,1)S(1)} copy-done((bf16[3,3,3,64,256]{4,3,2,1,0:T(8,128)(2,1)S(1)}, bf16[3,3,3,64,256]{4,3,2,1,0:T(8,128)(2,1)}, u32[]{:S(2)}) %copy-start) | copy-done | bytes 884760
  1.8 0.0 copy-start.1
  1.8 1.0 %copy-done.1 = bf16[3,3,3,128,64]{3,4,2,1,0:T(8,128)(2,1)S(1)} copy-done((bf16[3,3,3,128,64]{3,4,2,1,0:T(8,128)(2,1)S(1)}, bf16[3,3,3,128,64]{3,4,2,1,0:T(8,128)(2,1)}, u32[]{:S(2)}) %copy-start.1) | copy-done | bytes 442392
  2.8 0.0 copy-start.2
  2.8 0.8 %copy-done.2 = bf16[4,2,4,8,128]{4,3,2,1,0:T(8,128)(2,1)S(1)} copy-done((bf16[4,2,4,8,128]{4,3,2,1,0:T(8,128)(2,1)S(1)}, bf16[4,2,4,8,128]{4,3,2,1,0:T(8,128)(2,1)}, u32[]{:S(2)}) %copy-start.2) | copy-done | bytes 65560
  3.7 0.0 copy-start.3
  3.7 0.8 %copy-done.3 = f32[128,128]{1,0:T(8,128)S(1)} copy-done((f32[128,128]{1,0:T(8,128)S(1)}, f32[128,128]{1,0:T(8,128)}, u32[]{:S(2)}) %copy-start.3) | copy-done | bytes 65560
  4.5 0.0 copy-start.4
  4.5 0.7 %copy-done.4 = f32[4,4]{1,0:T(4,128)S(1)} copy-done((f32[4,4]{1,0:T(4,128)S(1)}, f32[4,4]{1,0:T(4,128)}, u32[]{:S(2)}) %copy-start.4) | copy-done | bytes 88
  5.2 13.5 %shard_map.101 = (bf16[8,4,2,4,8,128]{5,4,3,2,1,0:T(8,128)(2,1)S(1)}, f32[2,4,4]{2,1,0:T(4,128)S(1)}, bf16[27,128,128]{2,1,0:T(8,128)(2,1)S(1)}, bf16[27,128,256]{2,1,0:T(8,128)(2,1)S(1)}, f32[256,128]{1,0:T(8,128)S(1)}) custom-call(bf16[4,2,4,8,128]{4,3,2,1,0:T(8,128)(2,1)S(1)} %copy-done.2, f32[4,4]{1,0:T(4,128)S(1)} %copy-done.4, ...), custom_call_target="tpu_custom_call" | custom-call | tf_op jit(solution)/shard_map/pallas_call | solution.py:520
  18.7 0.0 copy-start.5
  18.7 0.7 %copy-done.5 = f32[128,4]{0,1:T(4,128)S(1)} copy-done((f32[128,4]{0,1:T(4,128)S(1)}, f32[128,4]{0,1:T(4,128)}, u32[]{:S(2)}) %copy-start.5) | copy-done | bytes 2072
  19.4 14.3 %shard_map.102 = (f32[27,64,128]{2,1,0:T(8,128)}, f32[27,64,256]{2,1,0:T(8,128)}, f32[128,128]{1,0:T(8,128)}, f32[4,128]{1,0:T(4,128)}, f32[1,1]{1,0:T(1,128)}) custom-call(bf16[8,4,2,4,8,128]{5,4,3,2,1,0:T(8,128)(2,1)S(1)} %get-tuple-element.15.volume_ref, f32[8,4]{1,0:T(8,128)S(1)} %bitcast.14, ...), custom_call_target="tpu_custom_call" | custom-call | tf_op jit(solution)/shard_map/pallas_call | solution.py:382
Async XLA Ops:
  0.6 1.2 %copy-start = (bf16[3,3,3,64,256]{4,3,2,1,0:T(8,128)(2,1)S(1)}, bf16[3,3,3,64,256]{4,3,2,1,0:T(8,128)(2,1)}, u32[]{:S(2)}) copy-start(bf16[3,3,3,64,256]{4,3,2,1,0:T(8,128)(2,1)} %param.9) | copy-start | bytes 2654212
  1.8 1.0 %copy-start.1 = (bf16[3,3,3,128,64]{3,4,2,1,0:T(8,128)(2,1)S(1)}, bf16[3,3,3,128,64]{3,4,2,1,0:T(8,128)(2,1)}, u32[]{:S(2)}) copy-start(bf16[3,3,3,128,64]{3,4,2,1,0:T(8,128)(2,1)} %param.8) | copy-start | bytes 1327108
  2.8 0.8 %copy-start.2 = (bf16[4,2,4,8,128]{4,3,2,1,0:T(8,128)(2,1)S(1)}, bf16[4,2,4,8,128]{4,3,2,1,0:T(8,128)(2,1)}, u32[]{:S(2)}) copy-start(bf16[4,2,4,8,128]{4,3,2,1,0:T(8,128)(2,1)} %volume_ref.1) | copy-start | bytes 196612
  3.7 0.8 %copy-start.3 = (f32[128,128]{1,0:T(8,128)S(1)}, f32[128,128]{1,0:T(8,128)}, u32[]{:S(2)}) copy-start(f32[128,128]{1,0:T(8,128)} %hidden_ref.1) | copy-start | bytes 196612
  4.5 0.7 %copy-start.4 = (f32[4,4]{1,0:T(4,128)S(1)}, f32[4,4]{1,0:T(4,128)}, u32[]{:S(2)}) copy-start(f32[4,4]{1,0:T(4,128)} %targets_ref.1) | copy-start | bytes 196
  18.7 0.7 %copy-start.5 = (f32[128,4]{0,1:T(4,128)S(1)}, f32[128,4]{0,1:T(4,128)}, u32[]{:S(2)}) copy-start(f32[128,4]{0,1:T(4,128)} %param.11) | copy-start | bytes 6148

commit v3 on v2

--- a/solution.py
+++ b/solution.py
@@ -186,10 +186,12 @@
 
 def whole_kernel(
     shape,
-    volume_ref, targets_ref, front_turned_ref, stride_ref, hidden_ref, output_ref,
+    gathered_hbm, targets_hbm, front_own_hbm, front_other_hbm, stride_own_hbm, stride_other_hbm,
+    hidden_hbm, output_hbm,
     grad_front_ref, grad_stride_ref, grad_hidden_ref, grad_output_ref, loss_ref,
     taps_ref, front_ref, act_ref, slope_ref, strided_ref, spread_ref, grad_pre_ref,
     front_out_ref, stride_out_ref, front_sem, stride_sem,
+    volume_ref, targets_ref, front_turned_ref, stride_ref, hidden_ref, output_ref, front_pre_ref, fetch_sem,
 ):
     slabs, batches, leading, thick, extent_x, extent_y, channels, inner = shape
     f32, bf16 = jnp.float32, jnp.bfloat16
@@ -203,8 +205,23 @@
     wide = 3 * channels
     local_rows = leading * extent_y
 
-    for tap in range(27):
-        front_ref[tap] = jnp.transpose(front_turned_ref[tap])
+    fetches = [
+        pltpu.make_async_copy(source, target, fetch_sem.at[i])
+        for i, (source, target) in enumerate(
+            [
+                (gathered_hbm, volume_ref),
+                (front_own_hbm, front_turned_ref.at[:, pl.ds(0, inner)]),
+                (front_other_hbm, front_turned_ref.at[:, pl.ds(inner, inner)]),
+                (stride_own_hbm, stride_ref.at[:, pl.ds(0, inner)]),
+                (stride_other_hbm, stride_ref.at[:, pl.ds(inner, inner)]),
+                (hidden_hbm, hidden_ref),
+                (output_hbm, output_ref),
+                (targets_hbm, targets_ref),
+            ]
+        )
+    ]
+    for fetch in fetches:
+        fetch.start()
 
     zeros = jnp.zeros((rows, wide), bf16)
     for x in range(extent_x + 2):
@@ -238,19 +255,38 @@
                 taps_ref[z + 1, x + 1, :, 2 * channels :] = high.astype(bf16)
         return carry
 
-    lax.fori_loop(0, slabs, fill, 0)
-
     half_zeros = jnp.zeros((half_rows, wide), bf16)
     for x in range(extent_x + 1):
         strided_ref[0, x] = half_zeros
+    front_pre_ref[1] = jnp.zeros((extent_x * rows, channels), f32)
+    fetches[0].wait()
+    lax.fori_loop(0, slabs, fill, 0)
+    fetches[1].wait()
+    fetches[2].wait()
+    for kz in range(3):
+        for tap in range(9):
+            front_ref[tap * channels : (tap + 1) * channels, kz * channels : (kz + 1) * channels] = jnp.transpose(
+                front_turned_ref[9 * kz + tap]
+            )
+
+    def front_taps(z, carry):
+        window = jnp.concatenate(
+            [taps_ref[z + 1, kx : kx + extent_x].reshape(extent_x * rows, wide) for kx in range(3)], axis=1
+        )
+        spread = jnp.dot(window, front_ref[...], preferred_element_type=f32)
+        front_pre_ref[z + 2] = spread[:, :channels]
+        front_pre_ref[z + 1] += spread[:, channels : 2 * channels]
+
+        @pl.when(z > 0)
+        def _():
+            front_pre_ref[z] += spread[:, 2 * channels :]
+
+        return carry
+
+    lax.fori_loop(0, depth, front_taps, 0)
 
     def front(z, carry):
-        total = jnp.zeros((extent_x * rows, channels), f32)
-        for kz in range(3):
-            for kx in range(3):
-                window = taps_ref[z + kz, kx : kx + extent_x].reshape(extent_x * rows, wide)
-                kernel = front_ref[3 * (3 * kz + kx) : 3 * (3 * kz + kx) + 3].reshape(wide, channels)
-                total += jnp.dot(window, kernel, preferred_element_type=f32)
+        total = front_pre_ref[z + 1]
         logistic = 1.0 / (1.0 + jnp.exp(-total))
         act = (total * logistic).astype(bf16).astype(f32)
         slope = logistic * (1.0 + total * (1.0 - logistic))
@@ -277,11 +313,10 @@
         start = 3 * (3 * kz + kx)
         return stride_ref[start : start + 3].reshape(wide, stride_ref.shape[-1])
 
-    pre = None
-    for kz in range(3):
-        for kx in range(3):
-            term = jnp.dot(strided_window(kz, kx), stride_kernel(kz, kx), preferred_element_type=f32)
-            pre = term if pre is None else pre + term
+    for fetch in fetches[3:]:
+        fetch.wait()
+    windows = jnp.concatenate([strided_window(kz, kx) for kz in range(3) for kx in range(3)], axis=1)
+    pre = jnp.dot(windows, stride_ref[...].reshape(27 * channels, stride_ref.shape[-1]), preferred_element_type=f32)
     logistic = 1.0 / (1.0 + jnp.exp(-pre))
     planes = half_z * half_x
     features = pre.shape[-1]
@@ -369,7 +404,7 @@
         send_out(front_out_ref, grad_front_ref, front_sem, group).wait()
 
 
-def whole_batch(shape, features, gathered, targets, front_all, stride_all, hidden_all, output_turned):
+def whole_batch(shape, features, gathered, targets, front_own, front_other, stride_own, stride_other, hidden_all, output_turned):
     slabs, batches, leading, thick, extent_x, extent_y, channels, inner = shape
     samples, depth = batches * leading, slabs * thick
     rows = samples * extent_y
@@ -388,11 +423,11 @@
             jax.ShapeDtypeStruct((outputs, hid), f32),
             jax.ShapeDtypeStruct((1, 1), f32),
         ),
-        in_specs=[vmem] * 6,
+        in_specs=[anywhere] * 8,
         out_specs=[anywhere] * 2 + [vmem] * 3,
         scratch_shapes=[
             pltpu.VMEM((depth + 2, extent_x + 2, rows, 3 * channels), bf16),
-            pltpu.VMEM((27, channels, channels), bf16),
+            pltpu.VMEM((9 * channels, 3 * channels), bf16),
             pltpu.VMEM((depth, extent_x, rows, channels), f32),
             pltpu.VMEM((depth, extent_x, rows, channels), f32),
             pltpu.VMEM((depth + 1, extent_x + 1, half_rows, 3 * channels), bf16),
@@ -402,22 +437,29 @@
             pltpu.VMEM((27, inner, features), f32),
             pltpu.SemaphoreType.DMA((9,)),
             pltpu.SemaphoreType.DMA((9,)),
+            pltpu.VMEM(gathered.shape, bf16),
+            pltpu.VMEM(targets.shape, f32),
+            pltpu.VMEM((27, channels, channels), bf16),
+            pltpu.VMEM((27, channels, features), bf16),
+            pltpu.VMEM(hidden_all.shape, f32),
+            pltpu.VMEM(output_turned.shape, f32),
+            pltpu.VMEM((depth + 2, extent_x * rows, channels), f32),
+            pltpu.SemaphoreType.DMA((8,)),
         ],
-        compiler_params=pltpu.CompilerParams(vmem_limit_bytes=40 << 20),
-    )(gathered, targets, front_all, stride_all, hidden_all, output_turned)
+        compiler_params=pltpu.CompilerParams(vmem_limit_bytes=60 << 20),
+    )(gathered, targets, front_own, front_other, stride_own, stride_other, hidden_all, output_turned)
 
 
 def gather_kernel(
     slabs, batches,
     volume_ref, targets_ref, front_ref, stride_ref, hidden_ref,
-    gathered_ref, targets_all_ref, front_all_ref, stride_all_ref, hidden_all_ref,
+    gathered_ref, targets_all_ref, front_other_ref, stride_other_ref, hidden_all_ref,
     local_sem, slab_sem, batch_sem, piece_sem, pair_send_sem, pair_sem,
     target_send_sem, target_sem, weight_send_sem, weight_sem,
 ):
     slab, batch, chan = lax.axis_index("slab"), lax.axis_index("batch"), lax.axis_index("chan")
     sibling = {"chan": 1 - chan}
     half = volume_ref.shape[0] // 2
-    inner = front_ref.shape[1]
     share = hidden_ref.shape[0]
 
     def remote(source, target, send_sem, recv_sem, device):
@@ -456,8 +498,8 @@
         send(remote(own, part(mine, chan), batch_sem.at[0, i], piece_sem.at[mine], device))
         send(remote(targets_ref, targets_all_ref.at[batch], target_send_sem.at[i], target_sem.at[batch], device))
     weights = [
-        remote(front_ref, front_all_ref.at[:, pl.ds(inner, inner)], weight_send_sem.at[0], weight_sem.at[0], sibling),
-        remote(stride_ref, stride_all_ref.at[:, pl.ds(inner, inner)], weight_send_sem.at[1], weight_sem.at[1], sibling),
+        remote(front_ref, front_other_ref, weight_send_sem.at[0], weight_sem.at[0], sibling),
+        remote(stride_ref, stride_other_ref, weight_send_sem.at[1], weight_sem.at[1], sibling),
         remote(hidden_ref, hidden_all_ref.at[pl.ds(chan * share, share)], weight_send_sem.at[2], weight_sem.at[2], sibling),
     ]
     for copy in weights:
@@ -465,9 +507,7 @@
     local = [
         pltpu.make_async_copy(volume_ref, gathered_ref.at[mine], local_sem.at[0]),
         pltpu.make_async_copy(targets_ref, targets_all_ref.at[batch], local_sem.at[1]),
-        pltpu.make_async_copy(front_ref, front_all_ref.at[:, pl.ds(0, inner)], local_sem.at[2]),
-        pltpu.make_async_copy(stride_ref, stride_all_ref.at[:, pl.ds(0, inner)], local_sem.at[3]),
-        pltpu.make_async_copy(hidden_ref, hidden_all_ref.at[pl.ds(chan * share, share)], local_sem.at[4]),
+        pltpu.make_async_copy(hidden_ref, hidden_all_ref.at[pl.ds(chan * share, share)], local_sem.at[2]),
     ]
     for copy in local:
         copy.start()
@@ -511,10 +551,7 @@
 def gather_inputs(volume, targets, front_turned, stride_own, hidden_weight):
     slabs, batches = lax.axis_size("slab"), lax.axis_size("batch")
     pieces = slabs * batches
-    vmem = pl.BlockSpec(memory_space=pltpu.VMEM)
-    hbm = pl.BlockSpec(memory_space=pltpu.HBM)
-    taps, inner, channels = front_turned.shape
-    features = stride_own.shape[-1]
+    anywhere = pl.BlockSpec(memory_space=pl.ANY)
     share, hid = hidden_weight.shape
     dma = pltpu.SemaphoreType.DMA
     return pl.pallas_call(
@@ -522,18 +559,18 @@
         out_shape=(
             jax.ShapeDtypeStruct((pieces,) + volume.shape, volume.dtype),
             jax.ShapeDtypeStruct((batches,) + targets.shape, targets.dtype),
-            jax.ShapeDtypeStruct((taps, 2 * inner, channels), front_turned.dtype),
-            jax.ShapeDtypeStruct((taps, 2 * inner, features), stride_own.dtype),
+            jax.ShapeDtypeStruct(front_turned.shape, front_turned.dtype),
+            jax.ShapeDtypeStruct(stride_own.shape, stride_own.dtype),
             jax.ShapeDtypeStruct((2 * share, hid), hidden_weight.dtype),
         ),
-        in_specs=[hbm] * 5,
-        out_specs=[vmem] * 5,
+        in_specs=[anywhere] * 5,
+        out_specs=[anywhere] * 5,
         scratch_shapes=[
-            dma((5,)), dma((slabs,)), dma((slabs, batches)), dma((pieces,)), dma((pieces,)), dma((pieces,)),
+            dma((3,)), dma((slabs,)), dma((slabs, batches)), dma((pieces,)), dma((pieces,)), dma((pieces,)),
             dma((batches,)), dma((batches,)), dma((3,)), dma((3,)),
         ],
         compiler_params=pltpu.CompilerParams(
-            collective_id=0, has_side_effects=True, vmem_limit_bytes=16 << 20
+            collective_id=0, has_side_effects=True, vmem_limit_bytes=60 << 20
         ),
     )(volume, targets, front_turned, stride_own, hidden_weight)
 
@@ -549,12 +586,12 @@
     shape = (slabs, batches) + volume.shape + (inner,)
     front_turned = jnp.swapaxes(front_weight.reshape(27, channels, inner), 1, 2)
     stride_own = stride_weight.reshape(27, inner, features)
-    gathered, targets, front_all, stride_all, hidden_all = gather_inputs(
+    gathered, targets, front_other, stride_other, hidden_all = gather_inputs(
         volume, targets, front_turned, stride_own, hidden_weight
     )
     grad_front, grad_stride, grad_hidden, grad_output, loss = whole_batch(
         shape, features, gathered, targets.reshape(-1, targets.shape[-1]),
-        front_all, stride_all, hidden_all, output_weight.T,
+        front_turned, front_other, stride_own, stride_other, hidden_all, output_weight.T,
     )
     return (
         jnp.swapaxes(grad_front, 1, 2).reshape(3, 3, 3, channels, inner),

time: 34.1 us -> 29.4 us (0.86)
  local copies, waits for them, and re-layouts: 5.21 us -> 0 us
  Pallas kernels: 27.9 us -> 28.6 us
    unnamed x12 -> x0, local copies, waits for them, and re-layouts: 5.21 us -> none
    pallas_call x1, Pallas kernels: 13.5 us -> 14.6 us  [gather_inputs(): pl.pallas_call(functools.partial(gather_kernel, slabs, batches), out_shap...]
where the time goes in v3:
time: 29.4 us; the launch traced here: 29.2 us
  Pallas kernels  28.6 us (97%)
  between operations  0.64 us (2%)
    pallas_call x1, Pallas kernels, gather_inputs(): pl.pallas_call(functools.partial(gather_kernel, slabs, batches), out_shap...  14.6 us
    pallas_call x1, Pallas kernels, whole_batch(): pl.pallas_call(functools.partial(whole_kernel, shape), out_shape=(jax.Sha...  14 us

profile of v3, /device:TPU:0, one launch (start us, length us, event | category | flops | bytes accessed | tf_op | source)
XLA Modules:
  0.0 29.2 jit_solution(173479580461065371)
XLA Ops:
  0.6 14.6 %shard_map.101 = (bf16[8,4,2,4,8,128]{5,4,3,2,1,0:T(8,128)(2,1)}, f32[2,4,4]{2,1,0:T(4,128)}, bf16[27,64,128]{2,1,0:T(8,128)(2,1)}, bf16[27,64,256]{2,1,0:T(8,128)(2,1)}, f32[256,128]{1,0:T(8,128)}) custom-call(bf16[4,2,4,8,128]{4,3,2,1,0:T(8,128)(2,1)} %volume_ref.1, f32[4,4]{1,0:T(4,128)} %targets_ref.1, bf16[27,64,128]{2,1,0:T(8,128)(2,1)} %bitcast.14, ...), custom_call_target="tpu_custom_call" | custom-call | tf_op jit(solution)/shard_map/pallas_call | solution.py:557
  15.2 14.0 %shard_map.102 = (f32[27,64,128]{2,1,0:T(8,128)}, f32[27,64,256]{2,1,0:T(8,128)}, f32[128,128]{1,0:T(8,128)}, f32[4,128]{1,0:T(4,128)}, f32[1,1]{1,0:T(1,128)}) custom-call(bf16[8,4,2,4,8,128]{5,4,3,2,1,0:T(8,128)(2,1)} %get-tuple-element.15.gathered_hbm, f32[8,4]{1,0:T(8,128)} %bitcast.16, bf16[27,64,128]{2,1,0:T(8,128)(2,1)} %bitcast.15, ...), custom_call_target="tpu_custom_call" | custom-call | tf_op jit(solution)/shard_map/pallas_call | solution.py:417

commit v4 on v3

--- a/solution.py
+++ b/solution.py
@@ -220,7 +220,7 @@
             ]
         )
     ]
-    for fetch in fetches:
+    for fetch in fetches[:3]:
         fetch.start()
 
     zeros = jnp.zeros((rows, wide), bf16)
@@ -260,6 +260,8 @@
         strided_ref[0, x] = half_zeros
     front_pre_ref[1] = jnp.zeros((extent_x * rows, channels), f32)
     fetches[0].wait()
+    for fetch in fetches[3:]:
+        fetch.start()
     lax.fori_loop(0, slabs, fill, 0)
     fetches[1].wait()
     fetches[2].wait()
@@ -355,16 +357,19 @@
     for kz in range(3):
         for kx in range(3):
             start = 3 * (3 * kz + kx)
-            spread = lax.dot_general(
-                grad_pre, stride_kernel(kz, kx), (((1,), (1,)), ((), ())), preferred_element_type=f32
-            )
-            spread_ref[3 * kz + kx] = spread.reshape(planes, half_rows, wide)
             kernel = lax.dot_general(
                 strided_window(kz, kx), grad_pre, (((0,), (0,)), ((), ())), preferred_element_type=f32
             )
             for ky in range(3):
                 stride_out_ref[start + ky] = kernel[ky * channels : ky * channels + inner]
             send_out(stride_out_ref, grad_stride_ref, stride_sem, 3 * kz + kx).start()
+
+    for kz in range(3):
+        for kx in range(3):
+            spread = lax.dot_general(
+                grad_pre, stride_kernel(kz, kx), (((1,), (1,)), ((), ())), preferred_element_type=f32
+            )
+            spread_ref[3 * kz + kx] = spread.reshape(planes, half_rows, wide)
 
     def sources(cell, half):
         if cell % 2 == 0:
@@ -391,13 +396,24 @@
 
     grads = grad_pre_ref[...].reshape(depth * extent_x * rows, channels).astype(bf16)
     grads = jnp.transpose(grads)[:inner]
-    for kz in range(3):
-        for kx in range(3):
-            window = taps_ref[kz : kz + depth, kx : kx + extent_x]
-            window = window.reshape(depth * extent_x * rows, wide)
-            turned = jnp.dot(grads, window, preferred_element_type=f32)
+    plane_cells = extent_x * rows
+    edge = jnp.zeros((inner, plane_cells), bf16)
+    stacked = jnp.concatenate(
+        [
+            jnp.concatenate([grads[:, plane_cells:], edge], axis=1),
+            grads,
+            jnp.concatenate([edge, grads[:, :-plane_cells]], axis=1),
+        ],
+        axis=0,
+    )
+    for kx in range(3):
+        window = taps_ref[1 : depth + 1, kx : kx + extent_x].reshape(depth * plane_cells, wide)
+        turned = jnp.dot(stacked, window, preferred_element_type=f32)
+        for kz in range(3):
             for ky in range(3):
-                front_out_ref[3 * (3 * kz + kx) + ky] = turned[:, ky * channels : (ky + 1) * channels]
+                front_out_ref[3 * (3 * kz + kx) + ky] = turned[
+                    kz * inner : (kz + 1) * inner, ky * channels : (ky + 1) * channels
+                ]
             send_out(front_out_ref, grad_front_ref, front_sem, 3 * kz + kx).start()
     for group in range(9):
         send_out(stride_out_ref, grad_stride_ref, stride_sem, group).wait()

time: 29.4 us -> 28.6 us (0.973)
  Pallas kernels: 28.6 us -> 27.8 us
    pallas_call x1, Pallas kernels: 14 us -> 13.2 us  [whole_batch(): pl.pallas_call(functools.partial(whole_kernel, shape), out_shape=(jax.Sha...]
where the time goes in v4:
time: 28.6 us; the launch traced here: 28.4 us
  Pallas kernels  27.8 us (97%)
  between operations  0.64 us (2%)
    pallas_call x1, Pallas kernels, gather_inputs(): pl.pallas_call(functools.partial(gather_kernel, slabs, batches), out_shap...  14.6 us
    pallas_call x1, Pallas kernels, whole_batch(): pl.pallas_call(functools.partial(whole_kernel, shape), out_shape=(jax.Sha...  13.2 us

profile of v4, /device:TPU:0, one launch (start us, length us, event | category | flops | bytes accessed | tf_op | source)
XLA Modules:
  0.0 28.4 jit_solution(8186004393274508024)
XLA Ops:
  0.6 14.6 %shard_map.101 = (bf16[8,4,2,4,8,128]{5,4,3,2,1,0:T(8,128)(2,1)}, f32[2,4,4]{2,1,0:T(4,128)}, bf16[27,64,128]{2,1,0:T(8,128)(2,1)}, bf16[27,64,256]{2,1,0:T(8,128)(2,1)}, f32[256,128]{1,0:T(8,128)}) custom-call(bf16[4,2,4,8,128]{4,3,2,1,0:T(8,128)(2,1)} %volume_ref.1, f32[4,4]{1,0:T(4,128)} %targets_ref.1, bf16[27,64,128]{2,1,0:T(8,128)(2,1)} %bitcast.14, ...), custom_call_target="tpu_custom_call" | custom-call | tf_op jit(solution)/shard_map/pallas_call | solution.py:573
  15.2 13.2 %shard_map.102 = (f32[27,64,128]{2,1,0:T(8,128)}, f32[27,64,256]{2,1,0:T(8,128)}, f32[128,128]{1,0:T(8,128)}, f32[4,128]{1,0:T(4,128)}, f32[1,1]{1,0:T(1,128)}) custom-call(bf16[8,4,2,4,8,128]{5,4,3,2,1,0:T(8,128)(2,1)} %get-tuple-element.15.gathered_hbm, f32[8,4]{1,0:T(8,128)} %bitcast.16, bf16[27,64,128]{2,1,0:T(8,128)(2,1)} %bitcast.15, ...), custom_call_target="tpu_custom_call" | custom-call | tf_op jit(solution)/shard_map/pallas_call | solution.py:433

commit v5 on v4

--- a/solution.py
+++ b/solution.py
@@ -466,6 +466,17 @@
     )(gathered, targets, front_own, front_other, stride_own, stride_other, hidden_all, output_turned)
 
 
+def partners(me, step, count):
+    if count & (count - 1):
+        return lax.rem(me + step, count), lax.rem(me + count - step, count)
+    other, bit = me, 1
+    while bit < count:
+        if step & bit:
+            other = other + bit - 2 * bit * ((me // bit) % 2)
+        bit *= 2
+    return other, other
+
+
 def gather_kernel(
     slabs, batches,
     volume_ref, targets_ref, front_ref, stride_ref, hidden_ref,
@@ -486,9 +497,9 @@
 
     slab_steps = range(1, slabs)
     batch_steps = range(1, batches)
-    to_slab = [{"slab": lax.rem(slab + step, slabs)} for step in slab_steps]
+    to_slab = [{"slab": partners(slab, step, slabs)[0]} for step in slab_steps]
     to_batch = [{"batch": lax.rem(batch + step, batches)} for step in batch_steps]
-    from_slab = [lax.rem(slab + slabs - step, slabs) for step in slab_steps]
+    from_slab = [partners(slab, step, slabs)[1] for step in slab_steps]
     from_batch = [lax.rem(batch + batches - step, batches) for step in batch_steps]
 
     barrier = pltpu.get_barrier_semaphore()

time: 28.6 us -> 28.6 us (level)
  no operation moved by 1% of the time
where the time goes in v5:
time: 28.6 us; the launch traced here: 28.4 us
  Pallas kernels  27.8 us (97%)
  between operations  0.64 us (2%)
    pallas_call x1, Pallas kernels, gather_inputs(): pl.pallas_call(functools.partial(gather_kernel, slabs, batches), out_shap...  14.6 us
    pallas_call x1, Pallas kernels, whole_batch(): pl.pallas_call(functools.partial(whole_kernel, shape), out_shape=(jax.Sha...  13.2 us

profile of v5, /device:TPU:0, one launch (start us, length us, event | category | flops | bytes accessed | tf_op | source)
XLA Modules:
  0.0 28.4 jit_solution(70005644356741657)
XLA Ops:
  0.6 14.6 %shard_map.101 = (bf16[8,4,2,4,8,128]{5,4,3,2,1,0:T(8,128)(2,1)}, f32[2,4,4]{2,1,0:T(4,128)}, bf16[27,64,128]{2,1,0:T(8,128)(2,1)}, bf16[27,64,256]{2,1,0:T(8,128)(2,1)}, f32[256,128]{1,0:T(8,128)}) custom-call(bf16[4,2,4,8,128]{4,3,2,1,0:T(8,128)(2,1)} %volume_ref.1, f32[4,4]{1,0:T(4,128)} %targets_ref.1, bf16[27,64,128]{2,1,0:T(8,128)(2,1)} %bitcast.14, ...), custom_call_target="tpu_custom_call" | custom-call | tf_op jit(solution)/shard_map/pallas_call | solution.py:584
  15.3 13.2 %shard_map.102 = (f32[27,64,128]{2,1,0:T(8,128)}, f32[27,64,256]{2,1,0:T(8,128)}, f32[128,128]{1,0:T(8,128)}, f32[4,128]{1,0:T(4,128)}, f32[1,1]{1,0:T(1,128)}) custom-call(bf16[8,4,2,4,8,128]{5,4,3,2,1,0:T(8,128)(2,1)} %get-tuple-element.15.gathered_hbm, f32[8,4]{1,0:T(8,128)} %bitcast.16, bf16[27,64,128]{2,1,0:T(8,128)(2,1)} %bitcast.15, ...), custom_call_target="tpu_custom_call" | custom-call | tf_op jit(solution)/shard_map/pallas_call | solution.py:433
